TPU v7x, 32 devices: a whole 2x2x4 slice. The times are simulated.
32 devices in a mesh: ka: 8 (over z, x), ga: 4 (over y, core).
Axes of the slice: x: 2, y: 2, z: 4, core: 2. Of those that a mesh axis runs over, the one named last changes fastest.
Arguments:
- coefficients: bfloat16 [8, 2, 256, 55296], P('ka', None, 'ga'), may hold values from -0.4375 to 0.4375
- shift_map: int32 [8, 3, 55296], P('ka', None, 'ga'), may hold values from 0 to 55295, as said below
- phase_angle: float32 [8, 3], P('ka'), may hold values from -3.140625 to 3.140625
Outputs:
- intersections: float32 [8, 3, 2, 256, 256], P('ka', None, None, 'ga')
Inputs may be any that keep to these rules, and one draw needn't show every extreme that they name: Each aligned block of 13824 consecutive entries of shift_map[k, b] is a permutation of the indices of that same block; it maps aligned tiles of 128 entries onto aligned tiles of 128 indices.
All inputs are finite; a program needn't handle non-finite values.
Results may differ from a plain program's by a relative error of at most 0.0003.
Values may be sent and summed in bfloat16 or wider, within the bound.
A program may use at most 192 MiB of HBM per device.

v0:
```python
import jax
import jax.numpy as jnp
from jax import lax
from jax.sharding import PartitionSpec as P


def passed_along(value, axis, steps):
    count = lax.axis_size(axis)
    pairs = [(source, (source + steps) % count) for source in range(count)]
    return lax.ppermute(value, axis, pairs)


def swapped(block, axis, bit):
    count = lax.axis_size(axis)
    route = []
    for low in range(count):
        high = low | 1 << bit
        if high != low and high < count:
            route += [(low, high), (high, low)]
    return lax.ppermute(block, axis, route)


def cross_terms(left, moved):
    prods = jnp.einsum("amg,bng->abmn", left, moved, preferred_element_type=jnp.float32)
    real_part = prods[0, 0] + prods[1, 1]
    imag_part = prods[0, 1] - prods[1, 0]
    return jnp.stack([real_part, imag_part])


def local(coefficients, shift_map, phase_angle):
    own = lax.all_to_all(coefficients, "ga", split_axis=3, concat_axis=2, tiled=True)
    next_x = passed_along(own, "ka", -4)
    next_y = swapped(own, "ka", 1)
    next_z = swapped(own, "ka", 0)
    block_width = own.shape[3]
    local_map = shift_map[0] - lax.axis_index("ga") * block_width
    left = own[0]
    movers = []
    for direction, other in enumerate((next_x, next_y, next_z)):
        movers.append(jnp.take(other[0], local_map[direction], axis=2))
    parts = jnp.stack([cross_terms(left, moved) for moved in movers])
    summed = lax.psum_scatter(
        jnp.transpose(parts, (2, 0, 1, 3)), "ga", scatter_dimension=0, tiled=True
    )
    summed = jnp.transpose(summed, (1, 2, 0, 3))
    real_part = summed[:, 0]
    imag_part = summed[:, 1]
    cosine = jnp.cos(phase_angle[0])[:, None, None]
    sine = jnp.sin(phase_angle[0])[:, None, None]
    rotated = jnp.stack(
        [cosine * real_part - sine * imag_part, sine * real_part + cosine * imag_part], axis=1
    )
    return rotated[None]


def solution(mesh):
    in_specs = (P("ka", None, "ga", None), P("ka", None, "ga"), P("ka", None))
    out_specs = P("ka", None, None, "ga", None)
    return jax.shard_map(local, mesh=mesh, in_specs=in_specs, out_specs=out_specs, check_vma=False)
```

profile of v0, /device:TPU:0, one launch (start us, length us, event | category | flops | bytes accessed | tf_op | source)
XLA Modules:
  0.0 1390.7 jit_solution(11480714659786665636)
XLA Ops:
  6.5 56.5 %copy.60 = bf16[1,2,64,55296]{2,1,0,3:T(2,128)(2,1)} copy(bf16[1,2,64,55296]{3,2,1,0:T(8,128)(2,1)} %param.5) | data formatting | bytes 28311552 | tf_op args[0]
  63.0 41.2 %reshape.175 = bf16[4,2,884736]{2,1,0:T(2,128)(2,1)} reshape(bf16[55296,1,2,64]{3,2,1,0:T(2,128)(2,1)} %bitcast.81) | data formatting | bytes 28311552
  104.3 165.8 %all_to_all.18 = bf16[4,2,884736]{2,1,0:T(2,128)(2,1)} all-to-all(bf16[4,2,884736]{2,1,0:T(2,128)(2,1)} %reshape.175), channel_id=1, replica_groups=mesh['ka'=8,'ga'=4] {'ga'}, dimensions={0} | all-to-all | bytes 28311552 | tf_op jit(solution)/shard_map/all_to_all | solution.py:31
  270.1 40.5 %reshape.176 = bf16[55296,1,2,64]{3,2,1,0:T(2,128)(2,1)} reshape(bf16[4,2,884736]{2,1,0:T(2,128)(2,1)} %all_to_all.18) | data formatting | bytes 28311552
  310.6 68.9 %copy.80 = bf16[1,2,64,4,13824]{4,3,2,1,0:T(4,128)(2,1)} copy(bf16[1,2,64,4,13824]{2,1,4,3,0:T(2,128)(2,1)} %bitcast.80) | data formatting | bytes 28311552 | tf_op jit(solution)/shard_map/all_to_all | solution.py:31
  379.5 16.3 %copy.62 = bf16[1,2,4,64,13824]{4,3,2,1,0:T(8,128)(2,1)} copy(bf16[1,2,4,64,13824]{4,2,3,1,0:T(4,128)(2,1)} %bitcast.86) | data formatting | bytes 28311552 | tf_op jit(solution)/shard_map/all_to_all | solution.py:31
  395.8 34.6 %copy.63 = bf16[1,2,256,13824]{2,1,3,0:T(2,128)(2,1)} copy(bf16[1,2,256,13824]{3,2,1,0:T(8,128)(2,1)} %bitcast.82) | data formatting | bytes 28311552 | tf_op jit(solution)/shard_map/all_to_all | solution.py:31
  430.4 2.1 collective-permute-start.2
  432.5 2.6 collective-permute-start
  437.4 299.1 %collective-permute-done.2 = bf16[1,2,256,13824]{2,1,3,0:T(2,128)(2,1)} collective-permute-done((bf16[1,2,256,13824]{2,1,3,0:T(2,128)(2,1)}, bf16[1,2,256,13824]{2,1,3,0:T(2,128)(2,1)}, u32[]{:S(2)}, u32[]{:S(2)}) %collective-permute-start.2) | collective-permute-done | bytes 14155808 | tf_op jit(solution)/shard_map/ppermute | solution.py:20
  736.5 55.4 %gather_fusion.2 = bf16[13824,2,256]{2,1,0:T(2,128)(2,1)} fusion(bf16[2,256,13824]{1,0,2:T(2,128)(2,1)} %bitcast.22, s32[14336]{0:T(1024)S(1)} %pad_clamp_fusion), kind=kCustom, calls=%fused_computation.2.clone | custom fusion | bytes 28366848 | tf_op jit(solution)/shard_map/jit(_take)/gather | solution.py:40
  791.9 52.0 %fusion.8 = bf16[2,256,13824]{1,0,2:T(2,128)(2,1)} fusion(bf16[13824,2,256]{2,1,0:T(2,128)(2,1)} %gather_fusion.2, pred[13824]{0:T(1024)(128)(4,1)S(1)} %compare_and_fusion), kind=kLoop, calls=%fused_computation.14 | loop fusion | flops 7077888 | bytes 28325376 | tf_op jit(solution)/shard_map/jit(_take)/select_n | solution.py:40
  843.9 34.9 %copy.72 = bf16[2,256,13824]{2,1,0:T(8,128)(2,1)} copy(bf16[2,256,13824]{1,0,2:T(2,128)(2,1)} %fusion.8) | data formatting | bytes 28311552 | tf_op jit(solution)/shard_map/jit(_take)/select_n | solution.py:40
  878.8 163.5 %collective-permute-done = bf16[1,2,256,13824]{2,1,3,0:T(2,128)(2,1)} collective-permute-done((bf16[1,2,256,13824]{2,1,3,0:T(2,128)(2,1)}, bf16[1,2,256,13824]{2,1,3,0:T(2,128)(2,1)}, u32[]{:S(2)}, u32[]{:S(2)}) %collective-permute-start) | collective-permute-done | bytes 14155808 | tf_op jit(solution)/shard_map/ppermute | solution.py:10
  1042.3 55.6 %gather_fusion = bf16[13824,2,256]{2,1,0:T(2,128)(2,1)} fusion(bf16[2,256,13824]{1,0,2:T(2,128)(2,1)} %bitcast.4, s32[14336]{0:T(1024)S(1)} %pad_clamp_fusion.2), kind=kCustom, calls=%fused_computation.clone | custom fusion | bytes 28366848 | tf_op jit(solution)/shard_map/jit(_take)/gather | solution.py:40
  1097.9 52.0 %fusion.6 = bf16[2,256,13824,1]{1,0,2,3:T(2,128)(2,1)} fusion(bf16[13824,2,256]{2,1,0:T(2,128)(2,1)} %gather_fusion, pred[13824]{0:T(1024)(128)(4,1)S(1)} %compare_and_fusion.2), kind=kLoop, calls=%fused_computation.12 | loop fusion | flops 7077888 | bytes 28325376 | tf_op jit(solution)/shard_map/jit(_take)/select_n | solution.py:40
  1150.0 14.8 %fusion.15 = f32[2,2,256,256]{2,3,0,1:T(8,128)S(1)} fusion(bf16[2,256,13824,1]{2,1,0,3:T(8,128)(2,1)} %bitcast.83, bf16[2,256,13824,1]{1,0,2,3:T(2,128)(2,1)} %fusion.6), kind=kOutput, calls=%fused_computation.18 | convolution fusion | flops 7247757312 | bytes 29360128 | tf_op jit(solution)/shard_map/amg,bng->abmn/dot_general | solution.py:24
  1164.8 14.8 %fusion.12 = f32[2,2,256,256]{2,3,1,0:T(8,128)S(1)} fusion(bf16[2,256,13824,1]{2,1,3,0:T(8,128)(2,1)} %bitcast.84, bf16[2,256,13824]{2,1,0:T(8,128)(2,1)} %copy.72), kind=kOutput, calls=%fused_computation.17 | convolution fusion | flops 7247757312 | bytes 29360128 | tf_op jit(solution)/shard_map/amg,bng->abmn/dot_general | solution.py:24
  1179.7 55.6 %gather_fusion.1 = bf16[13824,2,256]{2,1,0:T(2,128)(2,1)} fusion(bf16[2,256,13824]{1,0,2:T(2,128)(2,1)} %bitcast.13, s32[14336]{0:T(1024)S(1)} %pad_clamp_fusion.1), kind=kCustom, calls=%fused_computation.1.clone | custom fusion | bytes 28366848 | tf_op jit(solution)/shard_map/jit(_take)/gather | solution.py:40
  1235.3 52.0 %fusion.7 = bf16[2,256,13824]{1,0,2:T(2,128)(2,1)} fusion(bf16[13824,2,256]{2,1,0:T(2,128)(2,1)} %gather_fusion.1, pred[13824]{0:T(1024)(128)(4,1)S(1)} %compare_and_fusion.1), kind=kLoop, calls=%fused_computation.13 | loop fusion | flops 7077888 | bytes 28325376 | tf_op jit(solution)/shard_map/jit(_take)/select_n | solution.py:40
  1287.3 35.0 %copy.69 = bf16[2,256,13824]{2,1,0:T(8,128)(2,1)} copy(bf16[2,256,13824]{1,0,2:T(2,128)(2,1)} %fusion.7) | data formatting | bytes 28311552 | tf_op jit(solution)/shard_map/jit(_take)/select_n | solution.py:40
  1322.3 14.9 %fusion.9 = f32[2,2,256,256]{2,3,1,0:T(8,128)S(1)} fusion(bf16[2,256,13824,1]{2,1,3,0:T(8,128)(2,1)} %bitcast.85, bf16[2,256,13824]{2,1,0:T(8,128)(2,1)} %copy.69), kind=kOutput, calls=%fused_computation.16 | convolution fusion | flops 7247757312 | bytes 29360128 | tf_op jit(solution)/shard_map/amg,bng->abmn/dot_general | solution.py:24
  1337.6 2.1 copy.74
  1341.1 40.8 %all-reduce.3.cloned.1.call-done = f32[256,3,2,256]{3,2,1,0:T(2,128)} async-done(((f32[256,3,2,256]{3,2,1,0:T(2,128)}), f32[256,3,2,256]{3,2,1,0:T(2,128)}) %all-reduce.3.cloned.1.call-update) | async-done | bytes 1572880
  (34 shorter events, 5.3 us)
Async XLA Ops:
  6.5 1375.4 %all-reduce.3.cloned.1.call-start = ((), (), s32[]{:S(2)}) async-start(), calls=%async_computation.1 | async-start | bytes 3145728
  395.8 39.3 %copy-start = (s32[1,3,13824]{2,0,1:T(1,128)S(1)}, s32[1,3,13824]{2,0,1:T(1,128)}, u32[]{:S(2)}) copy-start(s32[1,3,13824]{2,0,1:T(1,128)} %param.6) | copy-start | bytes 497668
  430.4 306.1 %collective-permute-start.2 = (bf16[1,2,256,13824]{2,1,3,0:T(2,128)(2,1)}, bf16[1,2,256,13824]{2,1,3,0:T(2,128)(2,1)}, u32[]{:S(2)}, u32[]{:S(2)}) collective-permute-start(bf16[1,2,256,13824]{2,1,3,0:T(2,128)(2,1)} %copy.63), channel_id=1, source_target_pairs={{0,4},{4,0},{8,12},{12,8},{16,20},{20,16},{24,28},{28,24},{1,5},{5... | collective-permute-start | bytes 42467336 | tf_op jit(solution)/shard_map/ppermute | solution.py:20
  432.5 609.8 %collective-permute-start = (bf16[1,2,256,13824]{2,1,3,0:T(2,128)(2,1)}, bf16[1,2,256,13824]{2,1,3,0:T(2,128)(2,1)}, u32[]{:S(2)}, u32[]{:S(2)}) collective-permute-start(bf16[1,2,256,13824]{2,1,3,0:T(2,128)(2,1)} %copy.63), channel_id=1, source_target_pairs={{0,16},{4,20},{8,24},{12,28},{16,0},{20,4},{24,8},{28,12},{1,17},{... | collective-permute-start | bytes 42467336 | tf_op jit(solution)/shard_map/ppermute | solution.py:10
  435.5 744.2 %collective-permute-start.1 = (bf16[1,2,256,13824]{2,1,3,0:T(2,128)(2,1)}, bf16[1,2,256,13824]{2,1,3,0:T(2,128)(2,1)}, u32[]{:S(2)}, u32[]{:S(2)}) collective-permute-start(bf16[1,2,256,13824]{2,1,3,0:T(2,128)(2,1)} %copy.63), channel_id=1, source_target_pairs={{0,8},{8,0},{4,12},{12,4},{16,24},{24,16},{20,28},{28,20},{1,9},{9... | collective-permute-start | bytes 42467336 | tf_op jit(solution)/shard_map/ppermute | solution.py:20
  1322.3 17.5 %copy-start.2 = (u32[32]{0:T(128)S(1)}, u32[32]{0:T(128)}, u32[]{:S(2)}) copy-start(u32[32]{0:T(128)} %constant.21) | copy-start | bytes 388
  1322.3 18.7 %copy-start.1 = (f32[1,3]{1,0:T(1,128)S(1)}, f32[1,3]{1,0:T(1,128)}, u32[]{:S(2)}) copy-start(f32[1,3]{1,0:T(1,128)} %param.7) | copy-start | bytes 40
Sparse Core Ops, SparseCore 0:
  1339.9 41.9 all-reduce.2
where the time goes:
time: 1400 us; the launch traced here: 1390 us
  waiting for transfers between devices  503 us (36%)
  local copies, waits for them, and re-layouts  499 us (36%)
  blocking collectives  166 us (12%)
  other arithmetic  158 us (11%)
  matrix products  44.4 us (3%)
  between operations  14.3 us (1%)
    ppermute x2, waiting for transfers between devices, swapped(): return lax.ppermute(block, axis, route)  299 us
    gather x3, local copies, waits for them, and re-layouts, local(): movers.append(jnp.take(other[0], local_map[direction], axis=2))  167 us
    all_to_all x1, blocking collectives, local(): lax.all_to_all(coefficients, 'ga', split_axis=3, concat_axis=2, tiled=True)  166 us
    ppermute x1, waiting for transfers between devices, passed_along(): return lax.ppermute(value, axis, pairs)  163 us
    select_n x6, other arithmetic, local(): movers.append(jnp.take(other[0], local_map[direction], axis=2))  156 us
    unnamed x11, local copies, waits for them, and re-layouts  140 us
    all_to_all x3, local copies, waits for them, and re-layouts, local(): lax.all_to_all(coefficients, 'ga', split_axis=3, concat_axis=2, tiled=True)  120 us
    select_n x2, local copies, waits for them, and re-layouts, local(): movers.append(jnp.take(other[0], local_map[direction], axis=2))  69.9 us
  transfers between devices with their start and end apart: 4, of which 3 were waited for; matrix products, arithmetic and copies ran while one was open for 20% of the time, Pallas kernels for 0%

commit v1 on v0

--- a/solution.py
+++ b/solution.py
@@ -28,7 +28,10 @@
 
 
 def local(coefficients, shift_map, phase_angle):
-    own = lax.all_to_all(coefficients, "ga", split_axis=3, concat_axis=2, tiled=True)
+    own = jnp.concatenate(
+        lax.all_to_all(jnp.stack(jnp.split(coefficients, lax.axis_size("ga"), axis=3)), "ga", 0, 0),
+        axis=2,
+    )
     next_x = passed_along(own, "ka", -4)
     next_y = swapped(own, "ka", 1)
     next_z = swapped(own, "ka", 0)

time: 1400 us -> 1180 us (0.84)
  local copies, waits for them, and re-layouts: 499 us -> 287 us
    unnamed x11 -> x8, local copies, waits for them, and re-layouts: 140 us -> 1.65 us
    all_to_all x3 -> x1, local copies, waits for them, and re-layouts: 120 us -> 6.38 us  [local(): lax.all_to_all(jnp.stack(jnp.split(coefficients, lax.axis_size('ga'), axi...]
    reshape x0 -> x1, local copies, waits for them, and re-layouts: none -> 34.6 us  [local(): jnp.concatenate(lax.all_to_all(jnp.stack(jnp.split(coefficients, lax.axis...]
  transfers between devices with their start and end apart: 4 -> 4, of which waited for: 3 -> 3; matrix products, arithmetic and copies ran while one was open for 20% -> 24% of each run, Pallas kernels for 0% -> 0%
where the time goes in v1:
time: 1180 us
  waiting for transfers between devices  504 us (43%)
  local copies, waits for them, and re-layouts  287 us (24%)
  other arithmetic  161 us (14%)
  blocking collectives  159 us (13%)
  matrix products  44.5 us (4%)
  between operations  14.3 us (1%)
    ppermute x2, waiting for transfers between devices, swapped(): return lax.ppermute(block, axis, route)  299 us
    gather x3, local copies, waits for them, and re-layouts, local(): movers.append(jnp.take(other[0], local_map[direction], axis=2))  166 us
    ppermute x1, waiting for transfers between devices, passed_along(): return lax.ppermute(value, axis, pairs)  163 us
    all_to_all x1, blocking collectives, local(): lax.all_to_all(jnp.stack(jnp.split(coefficients, lax.axis_size('ga'), axi...  159 us
    select_n x6, other arithmetic, local(): movers.append(jnp.take(other[0], local_map[direction], axis=2))  156 us
    select_n x2, local copies, waits for them, and re-layouts, local(): movers.append(jnp.take(other[0], local_map[direction], axis=2))  70 us
    dot_general x3, matrix products, cross_terms(): jnp.einsum('amg,bng->abmn', left, moved, preferred_element_type=jnp.float32)  44.5 us
    unnamed x2, waiting for transfers between devices  41.1 us
  transfers between devices with their start and end apart: 4, of which 3 were waited for; matrix products, arithmetic and copies ran while one was open for 24% of the time, Pallas kernels for 0%

profile of v1, /device:TPU:0, one launch (start us, length us, event | category | flops | bytes accessed | tf_op | source)
XLA Modules:
  0.0 1175.4 jit_solution(581700691758890815)
XLA Ops:
  6.5 5.7 slice_bitcast_fusion.3
  12.2 3.2 pad_maximum_fusion
  15.4 158.9 %all_to_all.5 = bf16[4,1,2,64,13824]{4,3,2,1,0:T(8,128)(2,1)S(1)} all-to-all(bf16[4,1,2,64,13824]{4,3,2,1,0:T(8,128)(2,1)S(1)} %pad_maximum_fusion), channel_id=1, replica_groups=mesh['ka'=8,'ga'=4] {'ga'}, dimensions={0} | all-to-all | bytes 28311552 | tf_op jit(solution)/shard_map/all_to_all | solution.py:32
  174.3 6.4 copy.34
  180.7 34.6 %copy.35 = bf16[1,2,256,13824]{2,1,3,0:T(2,128)(2,1)} copy(bf16[1,2,256,13824]{3,2,1,0:T(8,128)(2,1)} %bitcast.87) | data formatting | bytes 28311552 | tf_op jit(solution)/shard_map/reshape | solution.py:31
  215.4 1.9 collective-permute-start.2
  217.3 2.6 collective-permute-start
  220.3 1.6 collective-permute-start.1
  222.1 299.1 %collective-permute-done.2 = bf16[1,2,256,13824]{2,1,3,0:T(2,128)(2,1)} collective-permute-done((bf16[1,2,256,13824]{2,1,3,0:T(2,128)(2,1)}, bf16[1,2,256,13824]{2,1,3,0:T(2,128)(2,1)}, u32[]{:S(2)}, u32[]{:S(2)}) %collective-permute-start.2) | collective-permute-done | bytes 14155808 | tf_op jit(solution)/shard_map/ppermute | solution.py:20
  521.2 55.4 %gather_fusion.2 = bf16[13824,2,256]{2,1,0:T(2,128)(2,1)} fusion(bf16[2,256,13824]{1,0,2:T(2,128)(2,1)} %bitcast.27, s32[14336]{0:T(1024)S(1)} %pad_clamp_fusion), kind=kCustom, calls=%fused_computation.2.clone | custom fusion | bytes 28366848 | tf_op jit(solution)/shard_map/jit(_take)/gather | solution.py:43
  576.6 52.0 %fusion.8 = bf16[2,256,13824]{1,0,2:T(2,128)(2,1)} fusion(bf16[13824,2,256]{2,1,0:T(2,128)(2,1)} %gather_fusion.2, pred[13824]{0:T(1024)(128)(4,1)S(1)} %compare_and_fusion), kind=kLoop, calls=%fused_computation.15 | loop fusion | flops 7077888 | bytes 28325376 | tf_op jit(solution)/shard_map/jit(_take)/select_n | solution.py:43
  628.7 35.0 %copy.43 = bf16[2,256,13824]{2,1,0:T(8,128)(2,1)} copy(bf16[2,256,13824]{1,0,2:T(2,128)(2,1)} %fusion.8) | data formatting | bytes 28311552 | tf_op jit(solution)/shard_map/jit(_take)/select_n | solution.py:43
  663.6 163.4 %collective-permute-done = bf16[1,2,256,13824]{2,1,3,0:T(2,128)(2,1)} collective-permute-done((bf16[1,2,256,13824]{2,1,3,0:T(2,128)(2,1)}, bf16[1,2,256,13824]{2,1,3,0:T(2,128)(2,1)}, u32[]{:S(2)}, u32[]{:S(2)}) %collective-permute-start) | collective-permute-done | bytes 14155808 | tf_op jit(solution)/shard_map/ppermute | solution.py:10
  827.1 55.4 %gather_fusion = bf16[13824,2,256]{2,1,0:T(2,128)(2,1)} fusion(bf16[2,256,13824]{1,0,2:T(2,128)(2,1)} %bitcast.7, s32[14336]{0:T(1024)S(1)} %pad_clamp_fusion.2), kind=kCustom, calls=%fused_computation.clone | custom fusion | bytes 28366848 | tf_op jit(solution)/shard_map/jit(_take)/gather | solution.py:43
  882.5 52.0 %fusion.6 = bf16[2,256,13824,1]{1,0,2,3:T(2,128)(2,1)} fusion(bf16[13824,2,256]{2,1,0:T(2,128)(2,1)} %gather_fusion, pred[13824]{0:T(1024)(128)(4,1)S(1)} %compare_and_fusion.2), kind=kLoop, calls=%fused_computation.13 | loop fusion | flops 7077888 | bytes 28325376 | tf_op jit(solution)/shard_map/jit(_take)/select_n | solution.py:43
  934.5 14.8 %fusion.15 = f32[2,2,256,256]{2,3,0,1:T(8,128)S(1)} fusion(bf16[2,256,13824,1]{2,1,0,3:T(8,128)(2,1)} %bitcast.88, bf16[2,256,13824,1]{1,0,2,3:T(2,128)(2,1)} %fusion.6), kind=kOutput, calls=%fused_computation.23 | convolution fusion | flops 7247757312 | bytes 29360128 | tf_op jit(solution)/shard_map/amg,bng->abmn/dot_general | solution.py:24
  949.4 14.8 %fusion.12 = f32[2,2,256,256]{2,3,1,0:T(8,128)S(1)} fusion(bf16[2,256,13824,1]{2,1,3,0:T(8,128)(2,1)} %bitcast.89, bf16[2,256,13824]{2,1,0:T(8,128)(2,1)} %copy.43), kind=kOutput, calls=%fused_computation.22 | convolution fusion | flops 7247757312 | bytes 29360128 | tf_op jit(solution)/shard_map/amg,bng->abmn/dot_general | solution.py:24
  964.3 55.4 %gather_fusion.1 = bf16[13824,2,256]{2,1,0:T(2,128)(2,1)} fusion(bf16[2,256,13824]{1,0,2:T(2,128)(2,1)} %bitcast.17, s32[14336]{0:T(1024)S(1)} %pad_clamp_fusion.1), kind=kCustom, calls=%fused_computation.1.clone | custom fusion | bytes 28366848 | tf_op jit(solution)/shard_map/jit(_take)/gather | solution.py:43
  1019.6 52.0 %fusion.7 = bf16[2,256,13824]{1,0,2:T(2,128)(2,1)} fusion(bf16[13824,2,256]{2,1,0:T(2,128)(2,1)} %gather_fusion.1, pred[13824]{0:T(1024)(128)(4,1)S(1)} %compare_and_fusion.1), kind=kLoop, calls=%fused_computation.14 | loop fusion | flops 7077888 | bytes 28325376 | tf_op jit(solution)/shard_map/jit(_take)/select_n | solution.py:43
  1071.6 35.0 %copy.40 = bf16[2,256,13824]{2,1,0:T(8,128)(2,1)} copy(bf16[2,256,13824]{1,0,2:T(2,128)(2,1)} %fusion.7) | data formatting | bytes 28311552 | tf_op jit(solution)/shard_map/jit(_take)/select_n | solution.py:43
  1106.6 14.9 %fusion.9 = f32[2,2,256,256]{2,3,1,0:T(8,128)S(1)} fusion(bf16[2,256,13824,1]{2,1,3,0:T(8,128)(2,1)} %bitcast.90, bf16[2,256,13824]{2,1,0:T(8,128)(2,1)} %copy.40), kind=kOutput, calls=%fused_computation.21 | convolution fusion | flops 7247757312 | bytes 29360128 | tf_op jit(solution)/shard_map/amg,bng->abmn/dot_general | solution.py:24
  1121.9 2.2 copy.45
  1125.4 41.1 %all-reduce.3.cloned.1.call-done = f32[256,3,2,256]{3,2,1,0:T(2,128)} async-done(((f32[256,3,2,256]{3,2,1,0:T(2,128)}), f32[256,3,2,256]{3,2,1,0:T(2,128)}) %all-reduce.3.cloned.1.call-update) | async-done | bytes 1572880
  1166.5 1.1 constant_dynamic-slice_fusion
  (32 shorter events, 2.6 us)
Async XLA Ops:
  6.5 1160.0 %all-reduce.3.cloned.1.call-start = ((), (), s32[]{:S(2)}) async-start(), calls=%async_computation.1 | async-start | bytes 3145728
  180.7 39.1 %copy-start = (s32[1,3,13824]{2,0,1:T(1,128)S(1)}, s32[1,3,13824]{2,0,1:T(1,128)}, u32[]{:S(2)}) copy-start(s32[1,3,13824]{2,0,1:T(1,128)} %param.6) | copy-start | bytes 497668
  215.4 305.9 %collective-permute-start.2 = (bf16[1,2,256,13824]{2,1,3,0:T(2,128)(2,1)}, bf16[1,2,256,13824]{2,1,3,0:T(2,128)(2,1)}, u32[]{:S(2)}, u32[]{:S(2)}) collective-permute-start(bf16[1,2,256,13824]{2,1,3,0:T(2,128)(2,1)} %copy.35), channel_id=1, source_target_pairs={{0,4},{4,0},{8,12},{12,8},{16,20},{20,16},{24,28},{28,24},{1,5},{5... | collective-permute-start | bytes 42467336 | tf_op jit(solution)/shard_map/ppermute | solution.py:20
  217.3 609.8 %collective-permute-start = (bf16[1,2,256,13824]{2,1,3,0:T(2,128)(2,1)}, bf16[1,2,256,13824]{2,1,3,0:T(2,128)(2,1)}, u32[]{:S(2)}, u32[]{:S(2)}) collective-permute-start(bf16[1,2,256,13824]{2,1,3,0:T(2,128)(2,1)} %copy.35), channel_id=1, source_target_pairs={{0,16},{4,20},{8,24},{12,28},{16,0},{20,4},{24,8},{28,12},{1,17},{... | collective-permute-start | bytes 42467336 | tf_op jit(solution)/shard_map/ppermute | solution.py:10
  220.3 744.0 %collective-permute-start.1 = (bf16[1,2,256,13824]{2,1,3,0:T(2,128)(2,1)}, bf16[1,2,256,13824]{2,1,3,0:T(2,128)(2,1)}, u32[]{:S(2)}, u32[]{:S(2)}) collective-permute-start(bf16[1,2,256,13824]{2,1,3,0:T(2,128)(2,1)} %copy.35), channel_id=1, source_target_pairs={{0,8},{8,0},{4,12},{12,4},{16,24},{24,16},{20,28},{28,20},{1,9},{9... | collective-permute-start | bytes 42467336 | tf_op jit(solution)/shard_map/ppermute | solution.py:20
  1106.6 17.5 %copy-start.2 = (u32[32]{0:T(128)S(1)}, u32[32]{0:T(128)}, u32[]{:S(2)}) copy-start(u32[32]{0:T(128)} %constant.21) | copy-start | bytes 388
  1106.6 18.8 %copy-start.1 = (f32[1,3]{1,0:T(1,128)S(1)}, f32[1,3]{1,0:T(1,128)}, u32[]{:S(2)}) copy-start(f32[1,3]{1,0:T(1,128)} %param.7) | copy-start | bytes 40
Sparse Core Ops, SparseCore 0:
  1124.2 42.2 all-reduce.2
